TPU v7x, 256 devices: a whole 4x4x8 slice. The times are simulated.
256 devices in a mesh: lat: 16 (over y, x), kpt: 16 (over z, core).
Axes of the slice: x: 4, y: 4, z: 8, core: 2. Of those that a mesh axis runs over, the one named last changes fastest.
Arguments:
- coarse: bfloat16 [2, 16, 256, 12288], P(None, 'lat', 'kpt'), may hold values from -0.1875 to 0.1875
- rp_vectors: int32 [16, 3], P('lat'), may hold values from -4 to 4
- rp_weights: int32 [16], P('lat'), may hold values from 1 to 3
- re_vectors: int32 [256, 3], replicated, may hold values from -4 to 4
- re_weights: int32 [256], replicated, may hold values from 1 to 3
- q_points: float32 [2, 3], replicated, may hold values from 0 to 1
- k_points: float32 [1024, 3], P('kpt'), may hold values from 0 to 1
- modes_rot: bfloat16 [2, 2, 48, 48], replicated, may hold values from -0.625 to 0.625
- u_k: bfloat16 [2, 1024, 16, 16], P(None, 'kpt'), may hold values from -1 to 1
- u_kq: bfloat16 [2, 2, 1024, 16, 16], P(None, None, 'kpt'), may hold values from -1 to 1
- mask_k: int32 [1024, 16], P('kpt'), may hold values 0 or 1
- mask_kq: int32 [2, 1024, 16], P(None, 'kpt'), may hold values 0 or 1
Outputs:
- coupling: bfloat16 [2, 1024, 2, 12288], P(None, 'kpt', None, 'lat')
All inputs are finite; a program needn't handle non-finite values. No bound on the sum of `mask_k` or of `mask_kq` on one device may be relied on, other than what follows from the above.
Results may differ from a plain program's by a relative error of at most 0.017.
Values may be sent and summed in bfloat16 or wider, within the bound.
No kernel may reach another device: no remote copies, remote signals or barrier semaphores. Data moves between devices by JAX's collectives and lax.ppermute only.
A program may use at most 64 MiB of HBM per device.

v0:
```python
import jax
import jax.numpy as jnp
from jax import lax
from jax.sharding import PartitionSpec as P

two_pi = 6.283185307179586


def phases(points, vectors, weights):
    cells = vectors.astype(jnp.float32)
    argument = two_pi * (
        points[:, 0:1] * cells[None, :, 0]
        + points[:, 1:2] * cells[None, :, 1]
        + points[:, 2:3] * cells[None, :, 2]
    )
    inverse = 1.0 / weights.astype(jnp.float32)
    return (
        (jnp.cos(argument) * inverse).astype(jnp.bfloat16),
        (jnp.sin(argument) * inverse).astype(jnp.bfloat16),
    )


def rotate_modes(values, modes_rot):
    shape = values.shape
    mode_count = modes_rot.shape[2]
    split = values.reshape(shape[0], shape[1], shape[2], mode_count, shape[3] // mode_count)
    br = jnp.einsum(
        "qmn,qrmx->qrnx", modes_rot[0], split[0], preferred_element_type=jnp.float32
    ) - jnp.einsum("qmn,qrmx->qrnx", modes_rot[1], split[1], preferred_element_type=jnp.float32)
    bi = jnp.einsum(
        "qmn,qrmx->qrnx", modes_rot[0], split[1], preferred_element_type=jnp.float32
    ) + jnp.einsum("qmn,qrmx->qrnx", modes_rot[1], split[0], preferred_element_type=jnp.float32)
    return jnp.stack([br, bi]).reshape(shape).astype(jnp.bfloat16)


def phonon_sum(block, vectors, weights, q_points):
    phase_real, phase_imag = phases(q_points, vectors, weights)
    rows = block.shape[1]
    cells = block.shape[2]
    lanes = block.shape[3]
    flat_real = block[0].reshape(rows, cells * lanes)
    flat_imag = block[1].reshape(rows, cells * lanes)
    part_real = jnp.dot(phase_real, flat_real, preferred_element_type=jnp.float32) - jnp.dot(
        phase_imag, flat_imag, preferred_element_type=jnp.float32
    )
    part_imag = jnp.dot(phase_real, flat_imag, preferred_element_type=jnp.float32) + jnp.dot(
        phase_imag, flat_real, preferred_element_type=jnp.float32
    )
    return jnp.stack([part_real, part_imag]).reshape(2, q_points.shape[0], cells, lanes)


def per_device(
    coarse,
    rp_vectors,
    rp_weights,
    re_vectors,
    re_weights,
    q_points,
    k_points,
    modes_rot,
    u_k,
    u_kq,
    mask_k,
    mask_kq,
):
    q_count = q_points.shape[0]
    k_count = k_points.shape[0]
    band_count = u_k.shape[2]
    partial_value = phonon_sum(coarse, rp_vectors, rp_weights, q_points)
    summed = lax.psum_scatter(partial_value, "lat", scatter_dimension=2, tiled=True).astype(
        jnp.bfloat16
    )
    rotated = rotate_modes(summed, modes_rot)
    shared = lax.all_to_all(rotated, "lat", split_axis=3, concat_axis=2, tiled=True)
    lane_local = shared.shape[3]
    portion = lax.all_gather(shared, "kpt", axis=2, tiled=True)
    kreal, kimag = phases(k_points, re_vectors, re_weights)
    er = jnp.einsum(
        "kr,qrx->kqx", kreal, portion[0], preferred_element_type=jnp.float32
    ) - jnp.einsum("kr,qrx->kqx", kimag, portion[1], preferred_element_type=jnp.float32)
    ei = jnp.einsum(
        "kr,qrx->kqx", kreal, portion[1], preferred_element_type=jnp.float32
    ) + jnp.einsum("kr,qrx->kqx", kimag, portion[0], preferred_element_type=jnp.float32)
    totals = jnp.stack([er, ei])
    mode_local = lane_local // (band_count * band_count)
    field = totals.astype(jnp.bfloat16).reshape(
        2, k_count, q_count, mode_local, band_count, band_count
    )
    tr = jnp.einsum(
        "kqmab,kbn->kqman", field[0], u_k[0], preferred_element_type=jnp.float32
    ) - jnp.einsum("kqmab,kbn->kqman", field[1], u_k[1], preferred_element_type=jnp.float32)
    ti = jnp.einsum(
        "kqmab,kbn->kqman", field[0], u_k[1], preferred_element_type=jnp.float32
    ) + jnp.einsum("kqmab,kbn->kqman", field[1], u_k[0], preferred_element_type=jnp.float32)
    tr = tr.astype(jnp.bfloat16)
    ti = ti.astype(jnp.bfloat16)
    outr = jnp.einsum(
        "qkac,kqman->kqmcn", u_kq[0], tr, preferred_element_type=jnp.float32
    ) + jnp.einsum("qkac,kqman->kqmcn", u_kq[1], ti, preferred_element_type=jnp.float32)
    outi = jnp.einsum(
        "qkac,kqman->kqmcn", u_kq[0], ti, preferred_element_type=jnp.float32
    ) - jnp.einsum("qkac,kqman->kqmcn", u_kq[1], tr, preferred_element_type=jnp.float32)
    window = (
        jnp.transpose(mask_kq.astype(jnp.float32), (1, 0, 2))[:, :, None, :, None]
        * mask_k.astype(jnp.float32)[:, None, None, None, :]
    )
    result = jnp.stack([outr * window, outi * window])
    return result.reshape(2, k_count, q_count, lane_local).astype(jnp.bfloat16)


def solution(mesh):
    placed = (
        P(None, "lat", "kpt", None),
        P("lat", None),
        P("lat"),
        P(),
        P(),
        P(),
        P("kpt", None),
        P(),
        P(None, "kpt", None, None),
        P(None, None, "kpt", None, None),
        P("kpt", None),
        P(None, "kpt", None),
    )
    return jax.shard_map(
        per_device,
        mesh=mesh,
        in_specs=placed,
        out_specs=P(None, "kpt", None, "lat"),
        check_vma=False,
    )
```

profile of v0, /device:TPU:1, one launch (start us, length us, event | category | flops | bytes accessed | tf_op | source)
XLA Modules:
  0.0 256.3 jit_solution(5092199044945277099)
XLA Ops:
  7.2 0.7 convert_element_type.53
  8.5 1.2 convert_bitcast_fusion.1
  10.4 2.1 convert_reduce_fusion.1
  12.4 1.5 multiply_subtract_fusion
  13.9 1.4 pad_maximum_fusion
  15.4 86.5 %all-reduce.2 = bf16[2,2,16,12288]{3,1,2,0:T(2,128)(2,1)} all-reduce(f32[2,2,16,12288]{3,1,2,0:T(2,128)S(1)} %pad_maximum_fusion), channel_id=2, replica_groups=mesh['lat'=16,'kpt'=16] {'lat'}, use_global_device_ids=true, to_apply=%region_0.0.clone | all-reduce | flops 786432 | bytes 4718592
  102.5 1.6 dynamic-slice_convert_fusion
  105.1 10.0 %copy.99 = bf16[2,2,1,12288]{1,0,2,3:T(2,128)(2,1)} copy(bf16[2,2,1,12288]{3,1,2,0:T(2,128)(2,1)S(1)} %pad_maximum_fusion.2) | data formatting | bytes 196608 | tf_op jit(solution)/shard_map/stack | solution.py:33
  115.1 13.7 %reshape.158 = bf16[16,2,1536]{2,1,0:T(2,128)(2,1)S(1)} reshape(bf16[12288,1,2,2]{3,2,1,0:T(2,128)(2,1)} %bitcast.147) | data formatting | bytes 196608
  128.8 9.2 %all_to_all.12 = bf16[16,2,1536]{2,1,0:T(2,128)(2,1)S(1)} all-to-all(bf16[16,2,1536]{2,1,0:T(2,128)(2,1)S(1)} %reshape.158), channel_id=1, replica_groups=mesh['lat'=16,'kpt'=16] {'lat'}, dimensions={0} | all-to-all | bytes 196608 | tf_op jit(solution)/shard_map/all_to_all | solution.py:74
  138.0 14.7 %reshape.159 = bf16[12288,1,2,2]{3,2,1,0:T(2,128)(2,1)} reshape(bf16[16,2,1536]{2,1,0:T(2,128)(2,1)S(1)} %all_to_all.12) | data formatting | bytes 196608
  152.8 9.9 %copy.128 = bf16[2,2,16,768]{3,2,1,0:T(8,128)(2,1)} copy(bf16[2,2,16,768]{1,0,3,2:T(2,128)(2,1)} %bitcast.148) | data formatting | bytes 196608 | tf_op jit(solution)/shard_map/all_to_all | solution.py:74
  163.0 1.0 copy.134
  164.0 1.5 copy.136
  165.5 1.5 copy.135
  167.1 0.7 broadcast_multiply_fusion
  167.8 45.9 %all-gather.2.cloned.1.call-done = bf16[2,2,256,768]{3,2,1,0:T(8,128)(2,1)} async-done(((bf16[2,2,16,768]{3,2,1,0:T(8,128)(2,1)}), bf16[2,2,256,768]{3,2,1,0:T(8,128)(2,1)}) %all-gather.2.cloned.1.call-update) | async-done | bytes 1572880 | tf_op jit(solution)/shard_map/all_gather | solution.py:76
  213.8 1.7 fusion.9
  215.5 1.6 fusion.1
  217.1 0.9 copy.104
  219.3 1.3 copy.103
  220.6 2.2 copy.106
  222.8 1.5 fusion.21
  226.8 2.4 fusion.10
  229.8 2.3 fusion.14
  232.1 2.3 fusion.12
  234.4 3.4 %copy.118 = f32[64,2,3,16,16]{0,3,4,2,1:T(8,128)} copy(f32[64,2,3,16,16]{4,3,2,1,0:T(8,128)} %fusion.10) | data formatting | bytes 786432 | tf_op jit(solution)/shard_map/qkac,kqman->kqmcn/dot_general | solution.py:102
  237.9 2.3 copy.113
  240.1 3.6 %copy.117 = f32[64,2,3,16,16]{0,3,4,2,1:T(8,128)} copy(f32[64,2,3,16,16]{4,3,2,1,0:T(8,128)} %fusion.14) | data formatting | bytes 786432 | tf_op jit(solution)/shard_map/qkac,kqman->kqmcn/dot_general | solution.py:100
  243.8 2.3 copy.114
  246.1 2.1 fusion.7
  248.3 1.1 copy.119
  (63 shorter events, 7.7 us)
Async XLA Ops:
  6.5 207.2 %all-gather.2.cloned.1.call-start = ((), (), s32[]{:S(2)}) async-start(), calls=%async_computation.1 | async-start | bytes 1671168 | tf_op jit(solution)/shard_map/all_gather | solution.py:76
  9.7 0.7 copy-start.10
  15.3 86.6 %copy-start.15 = (u32[256]{0:T(256)S(1)}, u32[256]{0:T(256)}, u32[]{:S(2)}) copy-start(u32[256]{0:T(256)} %constant.12) | copy-start | bytes 3076
  15.4 88.8 %copy-start.7 = (bf16[2,2,48,48]{3,2,1,0:T(8,128)(2,1)S(1)}, bf16[2,2,48,48]{3,2,1,0:T(8,128)(2,1)}, u32[]{:S(2)}) copy-start(bf16[2,2,48,48]{3,2,1,0:T(8,128)(2,1)} %param.19) | copy-start | bytes 55300
  152.7 9.9 %copy-start.12 = (s32[256,3]{0,1:T(4,128)S(1)}, s32[256,3]{0,1:T(4,128)}, u32[]{:S(2)}) copy-start(s32[256,3]{0,1:T(4,128)} %param.15) | copy-start | bytes 9220
  152.7 10.0 %copy-start.11 = (s32[64,16]{0,1:T(8,128)S(1)}, s32[64,16]{0,1:T(8,128)}, u32[]{:S(2)}) copy-start(s32[64,16]{0,1:T(8,128)} %param.22) | copy-start | bytes 12292
  152.8 10.0 %copy-start.8 = (bf16[2,64,16,16]{1,3,2,0:T(8,128)(2,1)S(1)}, bf16[2,64,16,16]{1,3,2,0:T(8,128)(2,1)}, u32[]{:S(2)}) copy-start(bf16[2,64,16,16]{1,3,2,0:T(8,128)(2,1)} %param.20) | copy-start | bytes 196612
  152.8 11.2 %copy-start.6 = (bf16[2,2,64,16,16]{2,4,3,1,0:T(8,128)(2,1)S(1)}, bf16[2,2,64,16,16]{2,4,3,1,0:T(8,128)(2,1)}, u32[]{:S(2)}) copy-start(bf16[2,2,64,16,16]{2,4,3,1,0:T(8,128)(2,1)} %param.21) | copy-start | bytes 393220
  162.6 4.4 %copy-start.14 = (s32[256]{0:T(256)S(1)}, s32[256]{0:T(256)}, u32[]{:S(2)}) copy-start(s32[256]{0:T(256)} %param.16) | copy-start | bytes 3076
  162.7 4.4 %copy-start.13 = (f32[64,3]{0,1:T(4,128)S(1)}, f32[64,3]{0,1:T(4,128)}, u32[]{:S(2)}) copy-start(f32[64,3]{0,1:T(4,128)} %param.18) | copy-start | bytes 2308
  162.7 4.5 %copy-start.9 = (s32[2,64,16]{1,2,0:T(8,128)S(1)}, s32[2,64,16]{1,2,0:T(8,128)}, u32[]{:S(2)}) copy-start(s32[2,64,16]{1,2,0:T(8,128)} %param.23) | copy-start | bytes 24580
  213.7 4.3 %copy-start.1 = (bf16[2,2,256,768]{3,2,1,0:T(8,128)(2,1)S(1)}, bf16[2,2,256,768]{3,2,1,0:T(8,128)(2,1)}, u32[]{:S(2)}) copy-start(bf16[2,2,256,768]{3,2,1,0:T(8,128)(2,1)} %all-gather.2.cloned.1.call-done) | copy-start | bytes 4718596
  224.8 1.0 copy-start.4
  225.8 1.0 copy-start.2
  226.8 2.4 copy-start.3
  240.1 3.6 %copy-start = (f32[64,2,3,16,16]{4,3,2,1,0:T(8,128)S(1)}, f32[64,2,3,16,16]{4,3,2,1,0:T(8,128)}, u32[]{:S(2)}) copy-start(f32[64,2,3,16,16]{4,3,2,1,0:T(8,128)} %fusion.12) | copy-start | bytes 1179652
  243.8 2.3 copy-start.5
Sparse Core Ops, SparseCore 0:
  162.8 50.9 all-gather.1
where the time goes:
time: 257 us; the launch traced here: 256 us
  blocking collectives  95.8 us (37%)
  local copies, waits for them, and re-layouts  74.4 us (29%)
  waiting for transfers between devices  45.9 us (18%)
  matrix products  15.8 us (6%)
  between operations  14.4 us (6%)
  other arithmetic  9.95 us (4%)
    unnamed x1, blocking collectives  86.5 us
    all_gather x1, waiting for transfers between devices, per_device(): portion = lax.all_gather(shared, 'kpt', axis=2, tiled=True)  45.9 us
    unnamed x41, local copies, waits for them, and re-layouts  34.8 us
    another operation x3, local copies, waits for them, and re-layouts, rotate_modes(): return jnp.stack([br, bi]).reshape(shape).astype(jnp.bfloat16)  10 us
    all_to_all x1, local copies, waits for them, and re-layouts, per_device(): lax.all_to_all(rotated, 'lat', split_axis=3, concat_axis=2, tiled=True)  9.89 us
    all_to_all x1, blocking collectives, per_device(): lax.all_to_all(rotated, 'lat', split_axis=3, concat_axis=2, tiled=True)  9.25 us
  transfers between devices with their start and end apart: 1, of which 1 were waited for; matrix products, arithmetic and copies ran while one was open for 2% of the time, Pallas kernels for 0%

commit v1 on v0

--- a/solution.py
+++ b/solution.py
@@ -71,7 +71,10 @@
         jnp.bfloat16
     )
     rotated = rotate_modes(summed, modes_rot)
-    shared = lax.all_to_all(rotated, "lat", split_axis=3, concat_axis=2, tiled=True)
+    shared = jnp.concatenate(
+        lax.all_to_all(jnp.stack(jnp.split(rotated, lax.axis_size("lat"), axis=3)), "lat", 0, 0),
+        axis=2,
+    )
     lane_local = shared.shape[3]
     portion = lax.all_gather(shared, "kpt", axis=2, tiled=True)
     kreal, kimag = phases(k_points, re_vectors, re_weights)

time: 257 us -> 209 us (0.81)
  local copies, waits for them, and re-layouts: 74.4 us -> 26.8 us
    unnamed x41 -> x39, local copies, waits for them, and re-layouts: 34.8 us -> 6.42 us
    another operation x3 -> x2, local copies, waits for them, and re-layouts: 10 us -> 0.04 us  [rotate_modes(): return jnp.stack([br, bi]).reshape(shape).astype(jnp.bfloat16)]
    all_to_all x1, local copies, waits for them, and re-layouts: 9.89 us -> 0.65 us  [per_device(): lax.all_to_all(jnp.stack(jnp.split(rotated, lax.axis_size('lat'), axis=3)...]
where the time goes in v1:
time: 209 us
  blocking collectives  95.8 us (46%)
  waiting for transfers between devices  45.9 us (22%)
  local copies, waits for them, and re-layouts  26.8 us (13%)
  matrix products  15.8 us (8%)
  between operations  14.5 us (7%)
  other arithmetic  10.1 us (5%)
    unnamed x1, blocking collectives  86.5 us
    all_gather x1, waiting for transfers between devices, per_device(): portion = lax.all_gather(shared, 'kpt', axis=2, tiled=True)  45.9 us
    all_to_all x1, blocking collectives, per_device(): lax.all_to_all(jnp.stack(jnp.split(rotated, lax.axis_size('lat'), axis=3)...  9.25 us
    unnamed x39, local copies, waits for them, and re-layouts  6.42 us
  transfers between devices with their start and end apart: 1, of which 1 were waited for; matrix products, arithmetic and copies ran while one was open for 2% of the time, Pallas kernels for 0%

profile of v1, /device:TPU:1, one launch (start us, length us, event | category | flops | bytes accessed | tf_op | source)
XLA Modules:
  0.0 208.8 jit_solution(9630728916496115983)
XLA Ops:
  7.2 0.7 convert_element_type.53
  7.8 0.6 fusion.57
  8.5 1.2 convert_bitcast_fusion.1
  10.4 2.1 convert_reduce_fusion.1
  12.4 1.5 multiply_subtract_fusion
  13.9 1.4 pad_maximum_fusion
  15.4 86.5 %all-reduce.2 = bf16[2,2,16,12288]{3,1,2,0:T(2,128)(2,1)} all-reduce(f32[2,2,16,12288]{3,1,2,0:T(2,128)S(1)} %pad_maximum_fusion), channel_id=3, replica_groups=mesh['lat'=16,'kpt'=16] {'lat'}, use_global_device_ids=true, to_apply=%region_0.0.clone | all-reduce | flops 786432 | bytes 4718592
  101.9 0.6 dynamic-slice
  102.5 1.6 dynamic-slice_convert_fusion
  105.3 9.2 %all_to_all.5 = bf16[16,2,2,1,768]{4,2,3,1,0:T(2,128)(2,1)S(1)} all-to-all(bf16[16,2,2,1,768]{4,2,3,1,0:T(2,128)(2,1)S(1)} %bitcast.259), channel_id=1, replica_groups=mesh['lat'=16,'kpt'=16] {'lat'}, dimensions={0} | all-to-all | bytes 196608 | tf_op jit(solution)/shard_map/all_to_all | solution.py:75
  114.6 0.7 copy.742
  115.6 1.0 copy.718
  116.6 1.5 copy.720
  118.1 1.5 copy.719
  119.7 0.7 broadcast_multiply_fusion
  120.4 45.9 %all-gather.3.cloned.1.call-done = bf16[2,2,256,1,768]{4,2,1,3,0:T(8,128)(2,1)} async-done(((bf16[2,2,16,1,768]{4,2,1,3,0:T(8,128)(2,1)}), bf16[2,2,256,1,768]{4,2,1,3,0:T(8,128)(2,1)}) %all-gather.3.cloned.1.call-update) | async-done | bytes 1572880 | tf_op jit(solution)/shard_map/all_gather | solution.py:79
  166.3 1.7 fusion.9
  168.1 1.6 fusion.1
  169.7 0.9 copy.689
  171.9 1.3 copy.688
  173.2 2.2 %copy.691 = bf16[64,2,3,16,16]{4,3,2,1,0:T(8,128)(2,1)S(1)} copy(bf16[64,2,3,16,16]{0,4,3,2,1:T(8,128)(2,1)} %bitcast.252) | data formatting | bytes 393216 | tf_op jit(solution)/shard_map/squeeze | solution.py:94
  175.3 1.5 fusion.21
  179.4 2.3 %fusion.10 = f32[64,2,3,16,16]{4,3,2,1,0:T(8,128)} fusion(bf16[64,2,3,16,16]{4,3,2,1,0:T(8,128)(2,1)S(1)} %subtract_convert_fusion, bf16[1,2,64,16,16]{4,3,1,2,0:T(8,128)(2,1)S(1)} %copy-done.2), kind=kOutput, calls=%fused_computation.26 | convolution fusion | flops 3145728 | bytes 655360 | tf_op jit(solution)/shard_map/qkac,kqman->kqmcn/dot_general | solution.py:105
  181.7 0.6 fusion.16
  182.4 2.3 %fusion.14 = f32[64,2,3,16,16]{4,3,2,1,0:T(8,128)} fusion(bf16[64,2,3,16,16]{4,3,2,1,0:T(8,128)(2,1)S(1)} %add_convert_fusion, bf16[1,2,64,16,16]{4,3,1,2,0:T(8,128)(2,1)S(1)} %copy-done.3), kind=kOutput, calls=%fused_computation.30 | convolution fusion | flops 3145728 | bytes 655360 | tf_op jit(solution)/shard_map/qkac,kqman->kqmcn/dot_general | solution.py:103
  184.7 2.3 %fusion.12 = f32[64,2,3,16,16]{4,3,2,1,0:T(8,128)} fusion(bf16[64,2,3,16,16]{4,3,2,1,0:T(8,128)(2,1)S(1)} %add_convert_fusion, bf16[1,2,64,16,16]{4,3,1,2,0:T(8,128)(2,1)S(1)} %copy-done.2), kind=kOutput, calls=%fused_computation.28 | convolution fusion | flops 3145728 | bytes 655360 | tf_op jit(solution)/shard_map/qkac,kqman->kqmcn/dot_general | solution.py:102
  187.0 3.4 %copy.703 = f32[64,2,3,16,16]{0,3,4,2,1:T(8,128)} copy(f32[64,2,3,16,16]{4,3,2,1,0:T(8,128)} %fusion.10) | data formatting | bytes 786432 | tf_op jit(solution)/shard_map/qkac,kqman->kqmcn/dot_general | solution.py:105
  190.4 2.3 %copy.698 = f32[64,2,3,16,16]{0,3,4,2,1:T(8,128)} copy(f32[64,2,3,16,16]{4,3,2,1,0:T(8,128)S(1)} %fusion.16) | data formatting | bytes 786432 | tf_op jit(solution)/shard_map/qkac,kqman->kqmcn/dot_general | solution.py:100
  192.7 3.6 %copy.702 = f32[64,2,3,16,16]{0,3,4,2,1:T(8,128)} copy(f32[64,2,3,16,16]{4,3,2,1,0:T(8,128)} %fusion.14) | data formatting | bytes 786432 | tf_op jit(solution)/shard_map/qkac,kqman->kqmcn/dot_general | solution.py:103
  196.3 2.3 %copy.699 = f32[64,2,3,16,16]{0,3,4,2,1:T(8,128)} copy(f32[64,2,3,16,16]{4,3,2,1,0:T(8,128)S(1)} %copy-done) | data formatting | bytes 786432 | tf_op jit(solution)/shard_map/qkac,kqman->kqmcn/dot_general | solution.py:102
  198.6 2.1 fusion.7
  200.9 1.1 copy.704
  (75 shorter events, 6.0 us)
Async XLA Ops:
  6.5 159.8 %all-gather.3.cloned.1.call-start = ((), (), s32[]{:S(2)}) async-start(), calls=%async_computation.1 | async-start | bytes 1671168 | tf_op jit(solution)/shard_map/all_gather | solution.py:79
  9.7 0.7 copy-start.10
  15.3 86.6 %copy-start.15 = (u32[256]{0:T(256)S(1)}, u32[256]{0:T(256)}, u32[]{:S(2)}) copy-start(u32[256]{0:T(256)} %constant.12) | copy-start | bytes 3076
  15.4 88.8 %copy-start.7 = (bf16[2,2,48,48]{3,2,1,0:T(8,128)(2,1)S(1)}, bf16[2,2,48,48]{3,2,1,0:T(8,128)(2,1)}, u32[]{:S(2)}) copy-start(bf16[2,2,48,48]{3,2,1,0:T(8,128)(2,1)} %param.19) | copy-start | bytes 55300
  104.2 11.0 %copy-start.12 = (s32[256,3]{0,1:T(4,128)S(1)}, s32[256,3]{0,1:T(4,128)}, u32[]{:S(2)}) copy-start(s32[256,3]{0,1:T(4,128)} %param.15) | copy-start | bytes 9220
  104.2 11.1 %copy-start.11 = (s32[64,16]{0,1:T(8,128)S(1)}, s32[64,16]{0,1:T(8,128)}, u32[]{:S(2)}) copy-start(s32[64,16]{0,1:T(8,128)} %param.22) | copy-start | bytes 12292
  104.2 11.1 %copy-start.8 = (bf16[2,64,16,16]{1,3,2,0:T(8,128)(2,1)S(1)}, bf16[2,64,16,16]{1,3,2,0:T(8,128)(2,1)}, u32[]{:S(2)}) copy-start(bf16[2,64,16,16]{1,3,2,0:T(8,128)(2,1)} %param.20) | copy-start | bytes 196612
  105.0 11.5 %copy-start.6 = (bf16[2,2,64,16,16]{2,4,3,1,0:T(8,128)(2,1)S(1)}, bf16[2,2,64,16,16]{2,4,3,1,0:T(8,128)(2,1)}, u32[]{:S(2)}) copy-start(bf16[2,2,64,16,16]{2,4,3,1,0:T(8,128)(2,1)} %param.21) | copy-start | bytes 393220
  114.6 5.1 %copy-start.14 = (s32[256]{0:T(256)S(1)}, s32[256]{0:T(256)}, u32[]{:S(2)}) copy-start(s32[256]{0:T(256)} %param.16) | copy-start | bytes 3076
  114.6 5.1 %copy-start.13 = (f32[64,3]{0,1:T(4,128)S(1)}, f32[64,3]{0,1:T(4,128)}, u32[]{:S(2)}) copy-start(f32[64,3]{0,1:T(4,128)} %param.18) | copy-start | bytes 2308
  114.6 5.1 %copy-start.9 = (s32[2,64,16]{1,2,0:T(8,128)S(1)}, s32[2,64,16]{1,2,0:T(8,128)}, u32[]{:S(2)}) copy-start(s32[2,64,16]{1,2,0:T(8,128)} %param.23) | copy-start | bytes 24580
  166.3 4.3 %copy-start.1 = (bf16[2,2,256,1,768]{4,2,1,3,0:T(8,128)(2,1)S(1)}, bf16[2,2,256,1,768]{4,2,1,3,0:T(8,128)(2,1)}, u32[]{:S(2)}) copy-start(bf16[2,2,256,1,768]{4,2,1,3,0:T(8,128)(2,1)} %all-gather.3.cloned.1.call-done) | copy-start | bytes 4718596
  177.4 1.0 copy-start.4
  178.3 1.0 copy-start.2
  179.4 2.4 %copy-start.3 = (bf16[1,2,64,16,16]{4,3,1,2,0:T(8,128)(2,1)S(1)}, bf16[1,2,64,16,16]{4,3,1,2,0:T(8,128)(2,1)}, u32[]{:S(2)}) copy-start(bf16[1,2,64,16,16]{4,3,1,2,0:T(8,128)(2,1)} %copy.719) | copy-start | bytes 196612
  192.7 3.6 %copy-start = (f32[64,2,3,16,16]{4,3,2,1,0:T(8,128)S(1)}, f32[64,2,3,16,16]{4,3,2,1,0:T(8,128)}, u32[]{:S(2)}) copy-start(f32[64,2,3,16,16]{4,3,2,1,0:T(8,128)} %fusion.12) | copy-start | bytes 1179652
  196.3 2.3 %copy-start.5 = (f32[64,2,16,16]{0,3,2,1:T(8,128)S(1)}, f32[64,2,16,16]{0,3,2,1:T(8,128)}, u32[]{:S(2)}) copy-start(f32[64,2,16,16]{0,3,2,1:T(8,128)} %broadcast_multiply_fusion) | copy-start | bytes 393220
Sparse Core Ops, SparseCore 0:
  115.4 50.9 all-gather.2
